TPU v7x, 32 devices: a whole 2x2x4 slice. The times are simulated.
32 devices in a mesh: dp: 4 (over z), vocab: 8 (over y, x, core).
Axes of the slice: x: 2, y: 2, z: 4, core: 2. Of those that a mesh axis runs over, the one named last changes fastest.
Arguments:
- packed_symbol_codes: int32 [32, 1024], P(('dp', 'vocab')), may hold values from 0 to 50256
- article_numbering: int32 [32, 1024], P(('dp', 'vocab')), may hold values from 0 to 19, never falling along the last dimension, each value on 1 to 256 neighbouring positions
- target_spots: int32 [32, 128], P(('dp', 'vocab')), may hold values from 0 to 1022
- answer_flags: int32 [32, 128], P(('dp', 'vocab')), may hold values 0 or 1
- shared_embedding: bfloat16 [50304, 1024], P('vocab'), may hold values from -0.6 to 0.6
- spot_embedding: bfloat16 [1024, 1024], replicated, may hold values from -0.359375 to 0.359375
- combined_qkv_weights: bfloat16 [1024, 3072], replicated, may hold values from -0.1875 to 0.1875
- attend_outgoing_weights: bfloat16 [1024, 1024], replicated, may hold values from -0.5 to 0.5
- dense_incoming_weights: bfloat16 [1024, 4096], replicated, may hold values from -0.1875 to 0.1875
- dense_outgoing_weights: bfloat16 [4096, 1024], replicated, may hold values from -0.09375 to 0.09375
- layernorm_affine: float32 [6, 1024], replicated, may hold values from -0.6 to 1.3, as said below
- bias_terms: float32 [9216], replicated, may hold values from -1.2 to 1.2
- adaptor_float_copies: float32 [73728], replicated, may hold values from -0.09375 to 0.09375
- average_moments: float32 [73728], replicated, may hold values from -1.2276159e-07 to 1.2276159e-07
- squared_moments: float32 [73728], replicated, may hold values from 1.3576945e-16 to 5.430778e-16
Outputs:
- refreshed_thin_pairs: float32 [73728], replicated
- updated_first_moment: float32 [73728], replicated
- updated_second_moment: float32 [73728], replicated
- gradient_global_norm: float32 [], replicated
- smoothed_entropy_cost: float32 [], replicated
Inputs may be any that keep to these rules, and one draw needn't show every extreme that they name: `article_numbering`: within a slot the document numbers never fall, every document has 1 to 256 tokens. `layernorm_affine`: rows 0 to 2 are gains, rows 3 to 5 shifts.
All inputs are finite; a program needn't handle non-finite values. No bound on the sum of `answer_flags` on one device may be relied on, other than what follows from the above.
Results may differ from a plain program's by a relative error of at most 0.00085.
The roundings to bfloat16 on the way count: a program that leaves them out, or rounds other values in their place, can miss the bound.
Values may be sent and summed in bfloat16 or wider, within the bound.
A program may use at most 320 MiB of HBM per device.

v0:
```python
from functools import partial
import math
import jax
import jax.numpy as jnp
from jax import lax
from jax.sharding import PartitionSpec as P

MODEL_WIDTH = 1024
HEADS = 16
FEEDFWD_UNITS = 4096
VOCAB_SIZE = 50257
RANK = 4
STEP = 10
ADAPTER_SCALE = 8.0
NORM_EPS = 1e-05
GRAD_CLIP = 0.0001
STRIDE_LENGTH = 0.02
BETA_ONE = 0.9
BETA_TWO = 0.999
SHRINK_PENALTY = 0.01
STABILITY_FLOOR = 1e-08
MASKED = -1e30


def matrix_multiply(left, right):
    return jnp.dot(left, right, preferred_element_type=jnp.float32)


def matrix_multiply_transposed_left(left, right):
    return lax.dot_general(
        left, right, (((0,), (0,)), ((), ())), preferred_element_type=jnp.float32
    )


def matrix_multiply_transposed_right(left, right):
    return lax.dot_general(
        left, right, (((1,), (1,)), ((), ())), preferred_element_type=jnp.float32
    )


def layer_norm(stream, gain, shift):
    centred = stream - jnp.mean(stream, axis=-1, keepdims=True)
    spread = lax.rsqrt(jnp.mean(centred * centred, axis=-1, keepdims=True) + NORM_EPS)
    return centred * spread * gain + shift


def positions(segments):
    steps_here = jnp.arange(segments.shape[0], dtype=jnp.int32)
    earlier = (segments[None, :] == segments[:, None]) & (steps_here[None, :] < steps_here[:, None])
    return jnp.sum(earlier.astype(jnp.int32), axis=1)


def distinct_thin_pairs(stacked_samples):
    shapes = [
        (MODEL_WIDTH, 3 * RANK),
        (3, RANK, MODEL_WIDTH),
        (MODEL_WIDTH, RANK),
        (RANK, MODEL_WIDTH),
        (MODEL_WIDTH, RANK),
        (RANK, FEEDFWD_UNITS),
        (FEEDFWD_UNITS, RANK),
        (RANK, MODEL_WIDTH),
    ]
    pieces = []
    offset = 0
    for shape in shapes:
        number = math.prod(shape)
        pieces.append(stacked_samples[offset : offset + number].reshape(shape))
        offset += number
    return pieces


def block_diagonal_mask(blocks):
    number, rank, width = blocks.shape
    eye = jnp.eye(number, dtype=blocks.dtype)
    return (eye[:, None, :, None] * blocks[:, :, None, :]).reshape(number * rank, number * width)


def select_rows(onehot, rows):
    return matrix_multiply(onehot, rows).astype(jnp.bfloat16)


def split_heads(rows):
    return rows.reshape(rows.shape[0], HEADS, rows.shape[1] // HEADS)


def logit_grads(masked_logits, log_total, hit, active_positions, row_weight, denom):
    grad_logits = (row_weight / denom)[:, None] * (
        jnp.exp(masked_logits - log_total[:, None])
        - 0.9 * hit.astype(jnp.float32)
        - 0.1 / VOCAB_SIZE * active_positions.astype(jnp.float32)[None, :]
    )
    return grad_logits.astype(jnp.bfloat16)


def adaptive_moment_update(grad, weight, first, second):
    first_new = BETA_ONE * first + (1.0 - BETA_ONE) * grad
    second_new = BETA_TWO * second + (1.0 - BETA_TWO) * grad * grad
    debiased_mean_estimate = first_new / (1.0 - BETA_ONE**STEP)
    debiased_variance_estimate = second_new / (1.0 - BETA_TWO**STEP)
    weight_new = weight - STRIDE_LENGTH * (
        debiased_mean_estimate / (jnp.sqrt(debiased_variance_estimate) + STABILITY_FLOOR)
        + SHRINK_PENALTY * weight
    )
    return (weight_new, first_new, second_new)


def local(
    packed_symbol_codes,
    article_numbering,
    target_spots,
    answer_flags,
    shared_embedding,
    spot_embedding,
    combined_qkv_weights,
    attend_outgoing_weights,
    dense_incoming_weights,
    dense_outgoing_weights,
    layernorm_affine,
    bias_terms,
    adaptor_float_copies,
    average_moments,
    squared_moments,
):
    tokens_here = packed_symbol_codes[0]
    segments = article_numbering[0]
    spot_objective = target_spots[0]
    rows_here = spot_objective.shape[0]
    shard_rows = shared_embedding.shape[0]
    table_base = lax.axis_index("vocab") * shard_rows
    all_tokens = lax.all_gather(packed_symbol_codes, "vocab", axis=0, tiled=True).reshape(-1)
    wanted = all_tokens - table_base
    inside = (wanted >= 0) & (wanted < shard_rows)
    picked = jnp.take(shared_embedding, jnp.clip(wanted, 0, shard_rows - 1), axis=0)
    embedded = lax.psum_scatter(
        jnp.where(inside[:, None], picked.astype(jnp.float32), 0.0).astype(jnp.bfloat16),
        "vocab",
        scatter_dimension=0,
        tiled=True,
    ).astype(jnp.float32)
    stream = embedded + jnp.take(spot_embedding, positions(segments), axis=0).astype(jnp.float32)
    a_qkv, b_qkv, a_o, b_o, a_fc, b_fc, a_p, b_p = [
        lexicon_portion.astype(jnp.bfloat16)
        for lexicon_portion in distinct_thin_pairs(adaptor_float_copies)
    ]
    width = stream.shape[1]
    hidden_width = dense_incoming_weights.shape[1]
    length = stream.shape[0]
    onehot = spot_objective[:, None] == jnp.arange(length, dtype=jnp.int32)[None, :]
    pick = onehot.astype(jnp.bfloat16)
    h1 = layer_norm(stream, layernorm_affine[0], layernorm_affine[3]).astype(jnp.bfloat16)
    stream_rows = jnp.take(stream, spot_objective, axis=0)
    h1_rows = select_rows(pick, h1)
    u1 = matrix_multiply(h1, a_qkv).astype(jnp.bfloat16)
    u1_rows = select_rows(pick, u1)
    q = (
        matrix_multiply(h1_rows, combined_qkv_weights[:, :width])
        + bias_terms[:width]
        + ADAPTER_SCALE * matrix_multiply(u1_rows[:, :RANK], b_qkv[0])
    ).astype(jnp.bfloat16)
    kv = (
        matrix_multiply(h1, combined_qkv_weights[:, width:])
        + bias_terms[width : 3 * width]
        + ADAPTER_SCALE * matrix_multiply(u1[:, RANK:], block_diagonal_mask(b_qkv[1:]))
    ).astype(jnp.bfloat16)
    queries, keys_all, values_all = (
        split_heads(q),
        split_heads(kv[:, :width]),
        split_heads(kv[:, width:]),
    )
    scale = queries.shape[2] ** (-0.5)
    there = jnp.arange(length, dtype=jnp.int32)[None, :]
    segment_rows = jnp.take(segments, spot_objective)
    allowed = (there <= spot_objective[:, None]) & (segment_rows[:, None] == segments[None, :])
    scores = (
        jnp.einsum("qhd,khd->hqk", queries, keys_all, preferred_element_type=jnp.float32) * scale
    )
    scores = jnp.where(allowed[None], scores, MASKED)
    top = jnp.max(scores, axis=2, keepdims=True)
    expd = jnp.exp(scores - top)
    probs = expd / jnp.sum(expd, axis=2, keepdims=True)
    probs_low = probs.astype(jnp.bfloat16)
    o = (
        jnp.einsum("hqk,khd->qhd", probs_low, values_all, preferred_element_type=jnp.float32)
        .reshape(rows_here, width)
        .astype(jnp.bfloat16)
    )
    uo = matrix_multiply(o, a_o).astype(jnp.bfloat16)
    middle = (
        stream_rows
        + matrix_multiply(o, attend_outgoing_weights)
        + bias_terms[3 * width : 4 * width]
        + ADAPTER_SCALE * matrix_multiply(uo, b_o)
    )
    h2, norm_two_back = jax.vjp(
        lambda value: layer_norm(value, layernorm_affine[1], layernorm_affine[4]), middle
    )
    h2 = h2.astype(jnp.bfloat16)
    uf = matrix_multiply(h2, a_fc).astype(jnp.bfloat16)
    pre = (
        matrix_multiply(h2, dense_incoming_weights)
        + bias_terms[4 * width : 4 * width + hidden_width]
        + ADAPTER_SCALE * matrix_multiply(uf, b_fc)
    )
    f, gelu_back = jax.vjp(partial(jax.nn.gelu, approximate=True), pre)
    f = f.astype(jnp.bfloat16)
    up = matrix_multiply(f, a_p).astype(jnp.bfloat16)
    output = (
        middle
        + matrix_multiply(f, dense_outgoing_weights)
        + bias_terms[4 * width + hidden_width :]
        + ADAPTER_SCALE * matrix_multiply(up, b_p)
    )
    closing_result, final_back = jax.vjp(
        lambda value: layer_norm(value, layernorm_affine[2], layernorm_affine[5]), output
    )
    final_rows = closing_result.astype(jnp.bfloat16)
    next_places = spot_objective + 1
    targets = jnp.take(tokens_here, next_places)
    weights_here = answer_flags[0] * (
        jnp.take(segments, spot_objective) == jnp.take(segments, next_places)
    ).astype(jnp.int32)
    all_labels = lax.all_gather(
        jnp.stack([targets, weights_here], axis=1), "vocab", axis=0, tiled=True
    )
    class_scores = matrix_multiply_transposed_right(
        lax.all_gather(final_rows, "vocab", axis=0, tiled=True), shared_embedding
    )
    vocab_ids = table_base + jnp.arange(shard_rows, dtype=jnp.int32)
    active_positions = vocab_ids < VOCAB_SIZE
    masked_logits = jnp.where(active_positions[None, :], class_scores, -jnp.inf)
    local_top = jnp.max(masked_logits, axis=1)
    smooth_local = jnp.sum(jnp.where(active_positions[None, :], class_scores, 0.0), axis=1)
    hit = vocab_ids[None, :] == all_labels[:, 0:1]
    target_local = jnp.sum(jnp.where(hit, class_scores, 0.0), axis=1)
    top = lax.pmax(local_top, "vocab")
    local_sum = jnp.sum(jnp.exp(masked_logits - top[:, None]), axis=1)
    exp_sum, smooth_sum, target_logit = lax.psum((local_sum, smooth_local, target_local), "vocab")
    log_total = top + jnp.log(exp_sum)
    row_weight = all_labels[:, 1].astype(jnp.float32)
    row_loss = log_total - 0.9 * target_logit - 0.1 * smooth_sum / VOCAB_SIZE
    loss_sum, weight_sum = lax.psum((jnp.sum(row_weight * row_loss), jnp.sum(row_weight)), "dp")
    denom = jnp.maximum(weight_sum, 1.0)
    smoothed_entropy_cost = loss_sum / denom
    grad_logits = logit_grads(masked_logits, log_total, hit, active_positions, row_weight, denom)
    grad_rows = lax.psum_scatter(
        matrix_multiply(
            lax.slice_in_dim(grad_logits, 0, rows_here * lax.axis_size("vocab"), axis=0),
            shared_embedding,
        ),
        "vocab",
        scatter_dimension=0,
        tiled=True,
    )
    same = spot_objective[:, None] == spot_objective[None, :]
    order = jnp.arange(rows_here, dtype=jnp.int32)
    repeat = jnp.any(same & (order[None, :] < order[:, None]), axis=1)
    merge = (same & ~repeat[:, None]).astype(jnp.float32)
    grad_final = jnp.dot(merge, grad_rows, precision=lax.Precision.HIGHEST)
    (dx3,) = final_back(grad_final)
    dm = dx3.astype(jnp.bfloat16)
    g_bp = ADAPTER_SCALE * matrix_multiply_transposed_left(up, dm)
    du_p = (ADAPTER_SCALE * matrix_multiply_transposed_right(dm, b_p)).astype(jnp.bfloat16)
    g_ap = matrix_multiply_transposed_left(f, du_p)
    df = matrix_multiply_transposed_right(
        dm, dense_outgoing_weights
    ) + matrix_multiply_transposed_right(du_p, a_p)
    (dpre,) = gelu_back(df)
    dpre = dpre.astype(jnp.bfloat16)
    g_bfc = ADAPTER_SCALE * matrix_multiply_transposed_left(uf, dpre)
    du_f = (ADAPTER_SCALE * matrix_multiply_transposed_right(dpre, b_fc)).astype(jnp.bfloat16)
    g_afc = matrix_multiply_transposed_left(h2, du_f)
    dh2 = matrix_multiply_transposed_right(
        dpre, dense_incoming_weights
    ) + matrix_multiply_transposed_right(du_f, a_fc)
    (grad_middle,) = norm_two_back(dh2)
    dx2 = dx3 + grad_middle
    da = dx2.astype(jnp.bfloat16)
    g_bo = ADAPTER_SCALE * matrix_multiply_transposed_left(uo, da)
    du_o = (ADAPTER_SCALE * matrix_multiply_transposed_right(da, b_o)).astype(jnp.bfloat16)
    g_ao = matrix_multiply_transposed_left(o, du_o)
    do = (
        matrix_multiply_transposed_right(da, attend_outgoing_weights)
        + matrix_multiply_transposed_right(du_o, a_o)
    ).astype(jnp.bfloat16)
    do = split_heads(do)
    dv = jnp.einsum("hqk,qhd->khd", probs_low, do, preferred_element_type=jnp.float32)
    dp = jnp.einsum("qhd,khd->hqk", do, values_all, preferred_element_type=jnp.float32)
    ds = (probs * (dp - jnp.sum(probs * dp, axis=2, keepdims=True))).astype(jnp.bfloat16)
    dq = jnp.einsum("hqk,khd->qhd", ds, keys_all, preferred_element_type=jnp.float32) * scale
    dk = jnp.einsum("hqk,qhd->khd", ds, queries, preferred_element_type=jnp.float32) * scale
    dq = dq.reshape(rows_here, width).astype(jnp.bfloat16)
    dk = dk.reshape(length, width).astype(jnp.bfloat16)
    dv = dv.reshape(length, width).astype(jnp.bfloat16)
    thirds = ((h1_rows, u1_rows, dq), (h1, u1, dk), (h1, u1, dv))
    g_bqkv = []
    g_aqkv = []
    for j, (normed, low, grad) in enumerate(thirds):
        low = low[:, j * RANK : (j + 1) * RANK]
        g_bqkv.append(ADAPTER_SCALE * matrix_multiply_transposed_left(low, grad))
        du = (ADAPTER_SCALE * matrix_multiply_transposed_right(grad, b_qkv[j])).astype(jnp.bfloat16)
        g_aqkv.append(matrix_multiply_transposed_left(normed, du))
    pieces = [
        jnp.concatenate(g_aqkv, axis=1),
        jnp.concatenate(g_bqkv, axis=0),
        g_ao,
        g_bo,
        g_afc,
        g_bfc,
        g_ap,
        g_bp,
    ]
    local_grad = jnp.concatenate([piece.reshape(-1) for piece in pieces])
    grad_total = lax.psum(local_grad, ("dp", "vocab"))
    gradient_global_norm = jnp.sqrt(jnp.sum(grad_total * grad_total))
    capped_derivative = grad_total * (GRAD_CLIP / jnp.maximum(gradient_global_norm, GRAD_CLIP))
    refreshed_thin_pairs, updated_first_moment, updated_second_moment = adaptive_moment_update(
        capped_derivative, adaptor_float_copies, average_moments, squared_moments
    )
    return (
        refreshed_thin_pairs,
        updated_first_moment,
        updated_second_moment,
        gradient_global_norm,
        smoothed_entropy_cost,
    )


def solution(mesh):
    return jax.shard_map(
        local,
        mesh=mesh,
        in_specs=(
            P(("dp", "vocab"), None),
            P(("dp", "vocab"), None),
            P(("dp", "vocab"), None),
            P(("dp", "vocab"), None),
            P("vocab", None),
            P(),
            P(),
            P(),
            P(),
            P(),
            P(),
            P(),
            P(),
            P(),
            P(),
        ),
        out_specs=(P(), P(), P(), P(), P()),
        check_vma=False,
    )
```

profile of v0, /device:TPU:8, one launch (start us, length us, event | category | flops | bytes accessed | tf_op | source)
XLA Modules:
  0.0 644.7 jit_solution(2936452298662439854)
XLA Ops:
  7.2 9.4 %all-gather = s32[8,1,1024]{2,1,0:T(1,128)S(1)} all-gather(s32[1,1,1024]{2,1,0:T(1,128)} %bitcast.159), channel_id=1, replica_groups=mesh['dp'=4,'vocab'=8] {'vocab'}, dimensions={0}, use_global_device_ids=true | all-gather | bytes 36864 | tf_op jit(solution)/shard_map/all_gather | solution.py:131
  16.9 47.0 %gather_fusion = bf16[8192,1024]{1,0:T(8,128)(2,1)} fusion(bf16[6288,1024]{1,0:T(8,128)(2,1)} %param.21, s32[8192]{0:T(1024)S(1)} %broadcast_clamp_fusion), kind=kCustom, calls=%fused_computation.3 | custom fusion | bytes 33587200 | tf_op jit(solution)/shard_map/jit(_take)/gather | solution.py:134
  63.9 15.2 %select_convert_fusion = bf16[8192,1024]{1,0:T(8,128)(2,1)} fusion(bf16[8192,1024]{1,0:T(8,128)(2,1)} %gather_fusion, pred[8192]{0:T(1024)(128)(4,1)S(1)} %compare_and_fusion.3, pred[8192]{0:T(1024)(128)(4,1)S(1)} %bitcast.197), kind=kLoop, calls=%fused_computation.7 | loop fusion | flops 33554432 | bytes 33570816 | tf_op jit(solution)/shard_map/convert_element_type | solution.py:136
  80.1 1.3 convert_element_type.189
  84.7 1.3 convert_element_type.200
  87.3 2.2 convert_element_type.208
  90.2 5.4 gather_fusion.1
  98.8 96.5 %reduce-scatter.3.cloned.1.call-done = bf16[1024,1024]{1,0:T(8,128)(2,1)} async-done(((bf16[8192,1024]{1,0:T(8,128)(2,1)}), bf16[1024,1024]{1,0:T(8,128)(2,1)}) %reduce-scatter.3.cloned.1.call-update) | async-done | bytes 2097168 | tf_op jit(solution)/shard_map/reduce_scatter | solution.py:135
  195.4 3.2 fusion.92
  201.2 1.5 copy-done.23
  203.9 6.8 %fusion.12 = f32[1024,2048]{1,0:T(8,128)} fusion(bf16[1024,1024]{1,0:T(8,128)(2,1)S(1)} %add_convert_fusion.1, bf16[1024,3072]{1,0:T(8,128)(2,1)S(1)} %bitcast.214), kind=kOutput, calls=%fused_computation.34 | convolution fusion | flops 4294967296 | bytes 14680064 | tf_op jit(solution)/shard_map/dot_general | solution.py:26
  211.6 4.8 add_convert_fusion
  216.4 2.5 fusion.93
  218.9 2.9 copy.44
  221.8 4.8 copy.46
  226.5 4.2 gather_fusion.2
  230.7 6.3 fusion.98
  237.6 6.1 fusion.44
  245.6 1.3 convolution_add_fusion.1
  247.0 2.4 multiply_convert_fusion.2
  249.9 1.4 fusion.40
  252.9 8.8 %all_gather.10 = s32[1024,2]{0,1:T(2,128)S(1)} all-gather(s32[128,2]{0,1:T(2,128)S(1)} %pad_add_fusion), channel_id=1, replica_groups=mesh['dp'=4,'vocab'=8] {'vocab'}, dimensions={0}, use_global_device_ids=true | all-gather | bytes 9216 | tf_op jit(solution)/shard_map/all_gather | solution.py:223
  263.0 17.9 %all-gather.3.cloned.1.call-done = bf16[1024,1024]{1,0:T(8,128)(2,1)} async-done(((bf16[128,1024]{1,0:T(8,128)(2,1)}), bf16[1024,1024]{1,0:T(8,128)(2,1)}) %all-gather.3.cloned.1.call-update) | async-done | bytes 2097168 | tf_op jit(solution)/shard_map/all_gather | solution.py:227
  280.8 23.6 %select_reduce_fusion.1 = (f32[1024]{0:T(1024)S(1)}, f32[1024,6288]{0,1:T(8,128)}) fusion(pred[6288]{0:T(1024)(128)(4,1)S(1)} %broadcast_compare_fusion, bf16[1024,1024]{1,0:T(8,128)(2,1)} %all-gather.3.cloned.1.call-done, bf16[6288,1024]{1,0:T(8,128)(2,1)} %param.21), kind=kOutput, calls=%fused_computation.17 | convolution fusion | flops 13199768576 | bytes 40741008 | tf_op jit(solution)/shard_map/dot_general | solution.py:36
  304.5 13.1 %pmax.7 = f32[1024]{0:T(1024)S(1)} all-reduce(f32[1024]{0:T(1024)S(1)} %get-tuple-element.61), channel_id=1, replica_groups=mesh['dp'=4,'vocab'=8] {'vocab'}, use_global_device_ids=true, to_apply=%region_14.16 | all-reduce | flops 1024 | bytes 8192 | tf_op jit(solution)/shard_map/pmax | solution.py:236
  317.6 12.1 %select_reduce_fusion = (f32[1024]{0:T(1024)S(1)}, f32[1024]{0:T(1024)S(1)}, f32[1024]{0:T(1024)S(1)}) fusion(f32[1024,6288]{0,1:T(8,128)} %get-tuple-element.62, pred[6288]{0:T(1024)(128)(4,1)S(1)} %broadcast_compare_fusion, f32[1024]{0:T(1024)S(1)} %pmax.7, s32[1024]{0:T(1024)S(1)} %bitcast.202, s32[6288]{0:T(1024)S(1)} %iota_add_fusion), kind=kLoop, calls=%fused_computation.15 | loop fusion | flops 51508224 | bytes 25807568 | tf_op jit(solution)/shard_map/reduce_sum | solution.py:233
  329.7 22.3 %all-reduce = (f32[1024]{0:T(1024)}, f32[1024]{0:T(1024)}, f32[1024]{0:T(1024)}) all-reduce(f32[1024]{0:T(1024)S(1)} %get-tuple-element.7, f32[1024]{0:T(1024)S(1)} %get-tuple-element.6, f32[1024]{0:T(1024)S(1)} %get-tuple-element.8), channel_id=1, replica_groups=mesh['dp'=4,'vocab'=8] {'vocab'}, use_global_device_ids=true, to_apply=%region_16.18 | all-reduce | flops 3072 | bytes 24576 | tf_op jit(solution)/shard_map/psum | solution.py:238
  352.0 1.3 multiply_reduce_fusion.7
  353.3 9.5 %all-reduce.1 = (f32[]{:T(128)}, f32[]{:T(128)}) all-reduce(f32[]{:T(128)} %fusion.88, f32[]{:T(128)} %get-tuple-element.21), channel_id=1, replica_groups=mesh['dp'=4,'vocab'=8] {'dp'}, use_global_device_ids=true, to_apply=%region_8.10 | all-reduce | flops 2 | bytes 16 | tf_op jit(solution)/shard_map/psum | solution.py:242
  363.5 28.8 %fusion.6 = f32[1024,1024]{1,0:T(8,128)} fusion(bf16[6288,1024]{1,0:T(8,128)(2,1)} %param.21, f32[1024,6288]{0,1:T(8,128)} %get-tuple-element.62, f32[6288]{0:T(1024)} %broadcast_select_fusion, s32[1024]{0:T(1024)S(1)} %bitcast.203, f32[1024]{0:T(1024)S(1)} %get-tuple-element.22, f32[1024]{0:T(1024)S(1)} %bitcast.212, s32[6288]{0:T(1024)S(1)} %iota_add_fusion, ...), kind=kOutput, calls=%fused_computation.18 | convolution fusion | flops 13238403072 | bytes 42896656 | tf_op jit(solution)/shard_map/dot_general | solution.py:26
  394.4 50.1 %reduce-scatter.5.cloned.1.call-done = f32[128,1024]{1,0:T(8,128)} async-done(((f32[1024,1024]{1,0:T(8,128)}), f32[128,1024]{1,0:T(8,128)}) %reduce-scatter.5.cloned.1.call-update) | async-done | bytes 524304 | tf_op jit(solution)/shard_map/reduce_scatter | solution.py:246
  444.5 1.6 multiply_reduce_fusion.3
  447.4 6.4 fusion.101
  453.8 1.8 fusion.106
  455.6 1.7 fusion.22
  458.1 2.9 fusion.102
  464.6 5.9 multiply_reduce_fusion
  471.2 1.6 multiply_convert_fusion
  472.8 1.5 fusion.41
  475.3 2.2 fusion.29
  477.6 1.9 fusion.58
  479.5 3.9 reshape.410
  486.4 2.2 convolution_multiply_fusion.9
  488.7 3.1 fusion.53
  491.8 3.0 fusion.52
  504.3 127.0 %all-reduce.4.cloned.1.call-done = f32[73728]{0:T(1024)} async-done(((f32[73728]{0:T(1024)}), f32[73728]{0:T(1024)}) %all-reduce.4.cloned.1.call-update) | async-done | bytes 294928 | tf_op jit(solution)/shard_map/psum | solution.py:314
  631.3 1.6 multiply_reduce_fusion.6
  633.7 2.0 multiply_subtract_fusion
  (285 shorter events, 41.2 us)
Async XLA Ops:
  7.2 83.0 %copy-start = (bf16[1024,1024]{1,0:T(8,128)(2,1)S(1)}, bf16[1024,1024]{1,0:T(8,128)(2,1)}, u32[]{:S(2)}) copy-start(bf16[1024,1024]{1,0:T(8,128)(2,1)} %param.22) | copy-start | bytes 6291460
  7.2 188.2 %reduce-scatter.3.cloned.1.call-start = ((), (), s32[]{:S(2)}) async-start(), calls=%async_computation.2 | async-start | bytes 18874368 | tf_op jit(solution)/shard_map/reduce_scatter | solution.py:135
  79.1 4.6 copy-start.3
  79.2 201.7 %all-gather.3.cloned.1.call-start = ((), (), s32[]{:S(2)}) async-start(), calls=%async_computation.3 | async-start | bytes 2359296 | tf_op jit(solution)/shard_map/all_gather | solution.py:227
  81.4 129.7 %copy-start.31 = (bf16[4,1024]{1,0:T(4,128)(2,1)}, bf16[4,1024]{1,0:T(4,128)(2,1)S(1)}, u32[]{:S(2)}) copy-start(bf16[4,1024]{1,0:T(4,128)(2,1)S(1)} %squeeze.21) | copy-start | bytes 24580
  90.1 5.4 copy-start.43
  90.2 6.0 copy-start.64
  90.2 6.6 %copy-start.34 = (f32[9216]{0:T(1024)S(1)}, f32[9216]{0:T(1024)}, u32[]{:S(2)}) copy-start(f32[9216]{0:T(1024)} %param.28) | copy-start | bytes 110596
  90.2 7.2 %copy-start.37 = (f32[6,1024]{1,0:T(8,128)S(1)}, f32[6,1024]{1,0:T(8,128)}, u32[]{:S(2)}) copy-start(f32[6,1024]{1,0:T(8,128)} %param.27) | copy-start | bytes 73732
  198.6 5.0 slice-start.10
  199.2 4.7 slice-start.11
  200.7 10.0 %copy-start.5 = (bf16[1024,1024]{1,0:T(8,128)(2,1)}, bf16[1024,1024]{1,0:T(8,128)(2,1)S(1)}, u32[]{:S(2)}) copy-start(bf16[1024,1024]{1,0:T(8,128)(2,1)S(1)} %add_convert_fusion.1) | copy-start | bytes 6291460
  202.7 8.0 %copy-start.20 = (bf16[128,1024]{1,0:T(8,128)(2,1)}, bf16[128,1024]{1,0:T(8,128)(2,1)S(1)}, u32[]{:S(2)}) copy-start(bf16[128,1024]{1,0:T(8,128)(2,1)S(1)} %convolution_convert_fusion) | copy-start | bytes 786436
  203.3 8.3 %copy-start.29 = (bf16[1024,12]{0,1:T(8,128)(2,1)}, bf16[1024,12]{0,1:T(8,128)(2,1)S(1)}, u32[]{:S(2)}) copy-start(bf16[1024,12]{0,1:T(8,128)(2,1)S(1)} %convolution_convert_fusion.1) | copy-start | bytes 73732
  203.9 7.3 %copy-start.53 = (bf16[128,12]{0,1:T(8,128)(2,1)}, bf16[128,12]{0,1:T(8,128)(2,1)S(1)}, u32[]{:S(2)}) copy-start(bf16[128,12]{0,1:T(8,128)(2,1)S(1)} %fusion.61) | copy-start | bytes 9220
  211.6 19.1 %copy-start.21 = (bf16[128,1024]{0,1:T(8,128)(2,1)}, bf16[128,1024]{0,1:T(8,128)(2,1)S(1)}, u32[]{:S(2)}) copy-start(bf16[128,1024]{0,1:T(8,128)(2,1)S(1)} %copy.45) | copy-start | bytes 786436
  221.8 8.9 %copy-start.7 = (bf16[1024,1024]{0,1:T(8,128)(2,1)}, bf16[1024,1024]{0,1:T(8,128)(2,1)S(1)}, u32[]{:S(2)}) copy-start(bf16[1024,1024]{0,1:T(8,128)(2,1)S(1)} %copy.44) | copy-start | bytes 6291460
  237.0 8.5 %slice-start.2 = ((s8[8388608]{0:T(1024)(128)(4,1)}), s8[4194304]{0:T(1024)(128)(4,1)S(1)}, s32[]{:S(2)}) async-start(s8[8388608]{0:T(1024)(128)(4,1)} %bitcast.163), calls=%async_computation.8 | async-start | bytes 8388608
  237.6 6.2 copy-start.11
  237.6 6.4 copy-start.9
  237.6 6.4 copy-start.17
  237.6 6.4 copy-start.41
  237.6 6.4 copy-start.61
  237.6 7.9 %slice-start.3 = ((s8[8388608]{0:T(1024)(128)(4,1)}), s8[4194304]{0:T(1024)(128)(4,1)S(1)}, s32[]{:S(2)}) async-start(s8[8388608]{0:T(1024)(128)(4,1)} %bitcast.163), calls=%async_computation.9 | async-start | bytes 8388608
  244.0 5.8 slice-start
  245.6 4.3 slice-start.1
  251.7 52.8 %copy-start.51 = (f32[128]{0:T(128)}, f32[128]{0:T(128)S(1)}, u32[]{:S(2)}) copy-start(f32[128]{0:T(128)S(1)} %broadcast_multiply_fusion.2) | copy-start | bytes 1540
  251.9 9.8 %copy-start.67 = (f32[128]{0:T(128)}, f32[128]{0:T(128)S(1)}, u32[]{:S(2)}) copy-start(f32[128]{0:T(128)S(1)} %multiply_reduce_fusion.4) | copy-start | bytes 1540
  251.9 9.8 %copy-start.59 = (f32[128]{0:T(128)}, f32[128]{0:T(128)S(1)}, u32[]{:S(2)}) copy-start(f32[128]{0:T(128)S(1)} %fusion.80) | copy-start | bytes 1540
  252.8 191.7 %reduce-scatter.5.cloned.1.call-start = ((), (), s32[]{:S(2)}) async-start(), calls=%async_computation.4 | async-start | bytes 4718592 | tf_op jit(solution)/shard_map/reduce_scatter | solution.py:246
  392.3 52.2 %copy-start.52 = (f32[128]{0:T(128)S(1)}, f32[128]{0:T(128)}, u32[]{:S(2)}) copy-start(f32[128]{0:T(128)} %copy-done.51) | copy-start | bytes 1540
  392.3 53.8 %copy-start.68 = (f32[128]{0:T(128)S(1)}, f32[128]{0:T(128)}, u32[]{:S(2)}) copy-start(f32[128]{0:T(128)} %copy-done.67) | copy-start | bytes 1540
  392.3 53.8 %copy-start.60 = (f32[128]{0:T(128)S(1)}, f32[128]{0:T(128)}, u32[]{:S(2)}) copy-start(f32[128]{0:T(128)} %copy-done.59) | copy-start | bytes 1540
  392.4 238.9 %all-reduce.4.cloned.1.call-start = ((), (), s32[]{:S(2)}) async-start(), calls=%async_computation.5 | async-start | bytes 589824 | tf_op jit(solution)/shard_map/psum | solution.py:314
  447.4 8.2 %copy-start.69 = (f32[128,4096]{1,0:T(8,128)S(1)}, f32[128,4096]{1,0:T(8,128)}, u32[]{:S(2)}) copy-start(f32[128,4096]{1,0:T(8,128)} %get-tuple-element.58) | copy-start | bytes 6291460
  447.4 10.5 %slice-start.4 = ((s8[8388608]{0:T(1024)(128)(4,1)}), s8[4194304]{0:T(1024)(128)(4,1)S(1)}, s32[]{:S(2)}) async-start(s8[8388608]{0:T(1024)(128)(4,1)} %bitcast.165), calls=%async_computation.10 | async-start | bytes 8388608
  464.6 5.9 copy-start.27
  464.6 5.9 slice-start.6
  464.6 6.5 %slice-start.7 = ((s8[8388608]{0:T(1024)(128)(4,1)}), s8[4194304]{0:T(1024)(128)(4,1)S(1)}, s32[]{:S(2)}) async-start(s8[8388608]{0:T(1024)(128)(4,1)} %bitcast.171), calls=%async_computation.13 | async-start | bytes 8388608
  475.3 10.4 %copy-start.6 = (bf16[16,64,1024]{2,1,0:T(8,128)(2,1)}, bf16[16,64,1024]{2,1,0:T(8,128)(2,1)S(1)}, u32[]{:S(2)}) copy-start(bf16[16,64,1024]{2,1,0:T(8,128)(2,1)S(1)} %multiply_convert_fusion.1) | copy-start | bytes 6291460
  477.5 8.3 %copy-start.30 = (bf16[1024,12]{0,1:T(8,128)(2,1)S(1)}, bf16[1024,12]{0,1:T(8,128)(2,1)}, u32[]{:S(2)}) copy-start(bf16[1024,12]{0,1:T(8,128)(2,1)} %copy-done.29) | copy-start | bytes 73732
  479.5 9.2 %copy-start.36 = (bf16[4,1024]{1,0:T(4,128)(2,1)S(1)}, bf16[4,1024]{1,0:T(4,128)(2,1)}, u32[]{:S(2)}) copy-start(bf16[4,1024]{1,0:T(4,128)(2,1)} %squeeze.25) | copy-start | bytes 24580
  485.7 6.1 copy-start.35
  488.7 6.1 copy-start.33
  488.7 147.0 %copy-start.1 = (bf16[1024,1024]{1,0:T(8,128)(2,1)S(1)}, bf16[1024,1024]{1,0:T(8,128)(2,1)}, u32[]{:S(2)}) copy-start(bf16[1024,1024]{1,0:T(8,128)(2,1)} %param.22) | copy-start | bytes 6291460
  491.8 141.9 %copy-start.19 = (f32[73728]{0:T(1024)S(1)}, f32[73728]{0:T(1024)}, u32[]{:S(2)}) copy-start(f32[73728]{0:T(1024)} %param.29) | copy-start | bytes 884740
  491.8 141.9 %copy-start.25 = (f32[73728]{0:T(1024)S(1)}, f32[73728]{0:T(1024)}, u32[]{:S(2)}) copy-start(f32[73728]{0:T(1024)} %param.30) | copy-start | bytes 884740
  491.8 141.9 %copy-start.26 = (f32[73728]{0:T(1024)S(1)}, f32[73728]{0:T(1024)}, u32[]{:S(2)}) copy-start(f32[73728]{0:T(1024)} %param.31) | copy-start | bytes 884740
  (38 other events, 80.1 us)
Sparse Core Ops, SparseCore 0:
  79.3 116.0 reduce-scatter.2
  252.9 27.8 all-gather.2
  392.5 51.9 reduce-scatter.4
  503.7 127.4 all-reduce.3
where the time goes:
time: 650 us; the launch traced here: 645 us
  waiting for transfers between devices  292 us (45%)
  matrix products  126 us (19%)
  local copies, waits for them, and re-layouts  98.7 us (15%)
  blocking collectives  63 us (10%)
  other arithmetic  45.7 us (7%)
  between operations  19.6 us (3%)
    psum x1, waiting for transfers between devices, local(): grad_total = lax.psum(local_grad, ('dp', 'vocab'))  127 us
    reduce_scatter x1, waiting for transfers between devices, local(): lax.psum_scatter(jnp.where(inside[:, None], picked.astype(jnp.float32), 0...  96.5 us
    reduce_scatter x1, waiting for transfers between devices, local(): lax.psum_scatter(matrix_multiply(lax.slice_in_dim(grad_logits, 0, rows_he...  50.1 us
    dot_general x17, matrix products, matrix_multiply(): return jnp.dot(left, right, preferred_element_type=jnp.float32)  49.7 us
    gather x1, local copies, waits for them, and re-layouts, local(): jnp.take(shared_embedding, jnp.clip(wanted, 0, shard_rows - 1), axis=0)  47 us
    dot_general x10, matrix products, matrix_multiply_transposed_right(): lax.dot_general(left, right, (((1,), (1,)), ((), ())), preferred_element_...  36.9 us
    psum x1, blocking collectives, local(): lax.psum((local_sum, smooth_local, target_local), 'vocab')  22.3 us
    all_gather x1, waiting for transfers between devices, local(): lax.all_gather(final_rows, 'vocab', axis=0, tiled=True)  17.9 us
  transfers between devices with their start and end apart: 4, of which 4 were waited for; matrix products, arithmetic and copies ran while one was open for 3% of the time, Pallas kernels for 0%

commit v1 on v0

--- a/solution.py
+++ b/solution.py
@@ -311,7 +311,7 @@
         g_bp,
     ]
     local_grad = jnp.concatenate([piece.reshape(-1) for piece in pieces])
-    grad_total = lax.psum(local_grad, ("dp", "vocab"))
+    grad_total = jnp.sum(lax.all_gather(local_grad, ("dp", "vocab")), axis=0)
     gradient_global_norm = jnp.sqrt(jnp.sum(grad_total * grad_total))
     capped_derivative = grad_total * (GRAD_CLIP / jnp.maximum(gradient_global_norm, GRAD_CLIP))
     refreshed_thin_pairs, updated_first_moment, updated_second_moment = adaptive_moment_update(

time: 650 us -> 608 us (0.935)
  waiting for transfers between devices: 292 us -> 247 us
    psum x1 -> x0, waiting for transfers between devices: 127 us -> none  [local(): grad_total = lax.psum(local_grad, ('dp', 'vocab'))]
    all_gather x0 -> x1, waiting for transfers between devices: none -> 81.5 us  [local(): grad_total = jnp.sum(lax.all_gather(local_grad, ('dp', 'vocab')), axis=0)]
    all_gather x0 -> x1, local copies, waits for them, and re-layouts: none -> 8.24 us  [local(): grad_total = jnp.sum(lax.all_gather(local_grad, ('dp', 'vocab')), axis=0)]
where the time goes in v1:
time: 608 us; the launch traced here: 602 us
  waiting for transfers between devices  247 us (41%)
  matrix products  127 us (21%)
  local copies, waits for them, and re-layouts  97.1 us (16%)
  blocking collectives  63 us (10%)
  other arithmetic  47.8 us (8%)
  between operations  19.9 us (3%)
    reduce_scatter x1, waiting for transfers between devices, local(): lax.psum_scatter(jnp.where(inside[:, None], picked.astype(jnp.float32), 0...  96.5 us
    all_gather x1, waiting for transfers between devices, local(): grad_total = jnp.sum(lax.all_gather(local_grad, ('dp', 'vocab')), axis=0)  81.5 us
    reduce_scatter x1, waiting for transfers between devices, local(): lax.psum_scatter(matrix_multiply(lax.slice_in_dim(grad_logits, 0, rows_he...  50.7 us
    dot_general x17, matrix products, matrix_multiply(): return jnp.dot(left, right, preferred_element_type=jnp.float32)  49.7 us
    gather x1, local copies, waits for them, and re-layouts, local(): jnp.take(shared_embedding, jnp.clip(wanted, 0, shard_rows - 1), axis=0)  47 us
    dot_general x10, matrix products, matrix_multiply_transposed_right(): lax.dot_general(left, right, (((1,), (1,)), ((), ())), preferred_element_...  36.6 us
    psum x1, blocking collectives, local(): lax.psum((local_sum, smooth_local, target_local), 'vocab')  22.3 us
    all_gather x1, waiting for transfers between devices, local(): lax.all_gather(final_rows, 'vocab', axis=0, tiled=True)  17.9 us
  transfers between devices with their start and end apart: 4, of which 4 were waited for; matrix products, arithmetic and copies ran while one was open for 3% of the time, Pallas kernels for 0%

profile of v1, /device:TPU:8, one launch (start us, length us, event | category | flops | bytes accessed | tf_op | source)
XLA Modules:
  0.0 601.5 jit_solution(9102648441063192562)
XLA Ops:
  7.2 9.4 %all-gather.1 = s32[8,1,1024]{2,1,0:T(1,128)S(1)} all-gather(s32[1,1,1024]{2,1,0:T(1,128)} %bitcast.159), channel_id=1, replica_groups=mesh['dp'=4,'vocab'=8] {'vocab'}, dimensions={0}, use_global_device_ids=true | all-gather | bytes 36864 | tf_op jit(solution)/shard_map/all_gather | solution.py:131
  16.9 47.0 %gather_fusion = bf16[8192,1024]{1,0:T(8,128)(2,1)} fusion(bf16[6288,1024]{1,0:T(8,128)(2,1)} %param.21, s32[8192]{0:T(1024)S(1)} %broadcast_clamp_fusion), kind=kCustom, calls=%fused_computation.3 | custom fusion | bytes 33587200 | tf_op jit(solution)/shard_map/jit(_take)/gather | solution.py:134
  63.9 15.2 %select_convert_fusion = bf16[8192,1024]{1,0:T(8,128)(2,1)} fusion(bf16[8192,1024]{1,0:T(8,128)(2,1)} %gather_fusion, pred[8192]{0:T(1024)(128)(4,1)S(1)} %compare_and_fusion.3, pred[8192]{0:T(1024)(128)(4,1)S(1)} %bitcast.197), kind=kLoop, calls=%fused_computation.7 | loop fusion | flops 33554432 | bytes 33570816 | tf_op jit(solution)/shard_map/convert_element_type | solution.py:136
  87.4 2.2 convert_element_type.208
  90.2 5.4 gather_fusion.1
  98.9 96.5 %reduce-scatter.3.cloned.1.call-done = bf16[1024,1024]{1,0:T(8,128)(2,1)} async-done(((bf16[8192,1024]{1,0:T(8,128)(2,1)}), bf16[1024,1024]{1,0:T(8,128)(2,1)}) %reduce-scatter.3.cloned.1.call-update) | async-done | bytes 2097168 | tf_op jit(solution)/shard_map/reduce_scatter | solution.py:135
  195.4 3.2 fusion.92
  201.2 1.5 copy-done.23
  203.9 6.8 %fusion.12 = f32[1024,2048]{1,0:T(8,128)} fusion(bf16[1024,1024]{1,0:T(8,128)(2,1)S(1)} %add_convert_fusion.1, bf16[1024,3072]{1,0:T(8,128)(2,1)S(1)} %bitcast.214), kind=kOutput, calls=%fused_computation.34 | convolution fusion | flops 4294967296 | bytes 14680064 | tf_op jit(solution)/shard_map/dot_general | solution.py:26
  211.6 4.8 add_convert_fusion
  216.4 2.5 fusion.93
  218.9 2.9 copy.44
  221.8 5.0 copy.46
  226.7 4.2 gather_fusion.2
  230.9 6.3 %fusion.98 = (f32[16,128]{1,0:T(8,128)S(1)}, f32[16,128,1024]{2,1,0:T(8,128)}) fusion(pred[128,1024]{1,0:T(8,128)(4,1)} %fusion.62, bf16[128,16,64]{0,2,1:T(8,128)(2,1)S(1)} %bitcast.182, bf16[1024,16,64]{0,2,1:T(8,128)(2,1)S(1)} %bitcast.169), kind=kOutput, calls=%fused_computation.217 | convolution fusion | flops 276825088 | bytes 10887168 | tf_op jit(solution)/shard_map/sub | solution.py:180
  237.8 6.1 %fusion.44 = bf16[16,64,128]{2,1,0:T(8,128)(2,1)S(1)} fusion(bf16[1024,16,64]{0,2,1:T(8,128)(2,1)} %bitcast.180, f32[16,128,1024]{2,1,0:T(8,128)} %get-tuple-element.54, f32[16,128]{1,0:T(8,128)S(1)} %get-tuple-element.53), kind=kOutput, calls=%fused_computation.79 | convolution fusion | flops 272760832 | bytes 10756096 | tf_op jit(solution)/shard_map/hqk,khd->qhd/dot_general | solution.py:184
  245.8 1.3 convolution_add_fusion.1
  247.2 2.4 multiply_convert_fusion.2
  250.1 1.4 fusion.40
  253.1 8.8 %all_gather.16 = s32[1024,2]{0,1:T(2,128)S(1)} all-gather(s32[128,2]{0,1:T(2,128)S(1)} %pad_add_fusion), channel_id=1, replica_groups=mesh['dp'=4,'vocab'=8] {'vocab'}, dimensions={0}, use_global_device_ids=true | all-gather | bytes 9216 | tf_op jit(solution)/shard_map/all_gather | solution.py:223
  263.2 17.9 %all-gather.5.cloned.1.call-done = bf16[1024,1024]{1,0:T(8,128)(2,1)} async-done(((bf16[128,1024]{1,0:T(8,128)(2,1)}), bf16[1024,1024]{1,0:T(8,128)(2,1)}) %all-gather.5.cloned.1.call-update) | async-done | bytes 2097168 | tf_op jit(solution)/shard_map/all_gather | solution.py:227
  281.0 23.4 %select_reduce_fusion.1 = (f32[1024]{0:T(1024)S(1)}, f32[1024,6288]{0,1:T(8,128)}) fusion(pred[6288]{0:T(1024)(128)(4,1)S(1)} %broadcast_compare_fusion, bf16[1024,1024]{1,0:T(8,128)(2,1)} %all-gather.5.cloned.1.call-done, bf16[6288,1024]{1,0:T(8,128)(2,1)} %param.21), kind=kOutput, calls=%fused_computation.17 | convolution fusion | flops 13199768576 | bytes 40741008 | tf_op jit(solution)/shard_map/dot_general | solution.py:36
  304.4 13.1 %pmax.7 = f32[1024]{0:T(1024)S(1)} all-reduce(f32[1024]{0:T(1024)S(1)} %get-tuple-element.61), channel_id=1, replica_groups=mesh['dp'=4,'vocab'=8] {'vocab'}, use_global_device_ids=true, to_apply=%region_14.16 | all-reduce | flops 1024 | bytes 8192 | tf_op jit(solution)/shard_map/pmax | solution.py:236
  317.5 12.1 %select_reduce_fusion = (f32[1024]{0:T(1024)S(1)}, f32[1024]{0:T(1024)S(1)}, f32[1024]{0:T(1024)S(1)}) fusion(f32[1024,6288]{0,1:T(8,128)} %get-tuple-element.62, pred[6288]{0:T(1024)(128)(4,1)S(1)} %broadcast_compare_fusion, f32[1024]{0:T(1024)S(1)} %pmax.7, s32[1024]{0:T(1024)S(1)} %bitcast.202, s32[6288]{0:T(1024)S(1)} %iota_add_fusion), kind=kLoop, calls=%fused_computation.15 | loop fusion | flops 51508224 | bytes 25807568 | tf_op jit(solution)/shard_map/reduce_sum | solution.py:233
  329.6 22.3 %all-reduce = (f32[1024]{0:T(1024)}, f32[1024]{0:T(1024)}, f32[1024]{0:T(1024)}) all-reduce(f32[1024]{0:T(1024)S(1)} %get-tuple-element.7, f32[1024]{0:T(1024)S(1)} %get-tuple-element.6, f32[1024]{0:T(1024)S(1)} %get-tuple-element.8), channel_id=1, replica_groups=mesh['dp'=4,'vocab'=8] {'vocab'}, use_global_device_ids=true, to_apply=%region_16.18 | all-reduce | flops 3072 | bytes 24576 | tf_op jit(solution)/shard_map/psum | solution.py:238
  352.0 1.3 multiply_reduce_fusion.7
  353.3 9.5 %all-reduce.1 = (f32[]{:T(128)}, f32[]{:T(128)}) all-reduce(f32[]{:T(128)} %fusion.88, f32[]{:T(128)} %get-tuple-element.21), channel_id=1, replica_groups=mesh['dp'=4,'vocab'=8] {'dp'}, use_global_device_ids=true, to_apply=%region_8.10 | all-reduce | flops 2 | bytes 16 | tf_op jit(solution)/shard_map/psum | solution.py:242
  363.4 28.9 %fusion.6 = f32[1024,1024]{1,0:T(8,128)} fusion(bf16[6288,1024]{1,0:T(8,128)(2,1)} %param.21, f32[1024,6288]{0,1:T(8,128)} %get-tuple-element.62, f32[6288]{0:T(1024)} %broadcast_select_fusion, s32[1024]{0:T(1024)S(1)} %bitcast.203, f32[1024]{0:T(1024)S(1)} %get-tuple-element.22, f32[1024]{0:T(1024)S(1)} %bitcast.212, s32[6288]{0:T(1024)S(1)} %iota_add_fusion, ...), kind=kOutput, calls=%fused_computation.18 | convolution fusion | flops 13238403072 | bytes 42896656 | tf_op jit(solution)/shard_map/dot_general | solution.py:26
  393.8 50.7 %reduce-scatter.5.cloned.1.call-done = f32[128,1024]{1,0:T(8,128)} async-done(((f32[1024,1024]{1,0:T(8,128)}), f32[128,1024]{1,0:T(8,128)}) %reduce-scatter.5.cloned.1.call-update) | async-done | bytes 524304 | tf_op jit(solution)/shard_map/reduce_scatter | solution.py:246
  444.5 1.6 multiply_reduce_fusion.3
  447.4 6.4 %fusion.101 = f32[128,4096]{1,0:T(8,128)S(1)} fusion(bf16[128,1024]{1,0:T(8,128)(2,1)S(1)} %add_convert_fusion.5, bf16[4096,1024]{1,0:T(8,128)(2,1)} %param.26), kind=kOutput, calls=%fused_computation.220 | convolution fusion | flops 1073741824 | bytes 10747904 | tf_op jit(solution)/shard_map/dot_general | solution.py:36
  453.8 1.8 fusion.106
  455.6 1.7 fusion.22
  458.0 2.9 fusion.102
  464.6 5.9 multiply_reduce_fusion
  471.2 1.6 multiply_convert_fusion
  472.8 1.5 fusion.41
  474.4 2.1 multiply_convert_fusion.1
  476.5 2.2 fusion.29
  478.8 1.4 fusion.58
  480.2 3.2 reshape.410
  484.0 2.2 convolution_multiply_fusion.10
  486.3 2.2 convolution_multiply_fusion.9
  488.6 2.3 fusion.53
  490.9 2.3 fusion.52
  495.3 81.5 %all-gather.7.cloned.1.call-done = f32[2359296]{0:T(1024)} async-done(((f32[73728]{0:T(1024)}), f32[2359296]{0:T(1024)}) %all-gather.7.cloned.1.call-update) | async-done | bytes 9437200 | tf_op jit(solution)/shard_map/all_gather | solution.py:314
  576.9 8.2 %reshape.460 = f32[32,73728]{1,0:T(8,128)} reshape(f32[2359296]{0:T(1024)} %all-gather.7.cloned.1.call-done) | data formatting | bytes 18874368 | tf_op jit(solution)/shard_map/all_gather | solution.py:314
  585.1 4.7 reduce_sum.214
  (287 shorter events, 34.1 us)
Async XLA Ops:
  7.2 83.0 %copy-start = (bf16[1024,1024]{1,0:T(8,128)(2,1)S(1)}, bf16[1024,1024]{1,0:T(8,128)(2,1)}, u32[]{:S(2)}) copy-start(bf16[1024,1024]{1,0:T(8,128)(2,1)} %param.22) | copy-start | bytes 6291460
  7.2 188.2 %reduce-scatter.3.cloned.1.call-start = ((), (), s32[]{:S(2)}) async-start(), calls=%async_computation.2 | async-start | bytes 18874368 | tf_op jit(solution)/shard_map/reduce_scatter | solution.py:135
  79.1 4.7 copy-start.3
  79.2 201.9 %all-gather.5.cloned.1.call-start = ((), (), s32[]{:S(2)}) async-start(), calls=%async_computation.3 | async-start | bytes 2359296 | tf_op jit(solution)/shard_map/all_gather | solution.py:227
  81.4 129.7 %copy-start.31 = (bf16[4,1024]{1,0:T(4,128)(2,1)}, bf16[4,1024]{1,0:T(4,128)(2,1)S(1)}, u32[]{:S(2)}) copy-start(bf16[4,1024]{1,0:T(4,128)(2,1)S(1)} %squeeze.21) | copy-start | bytes 24580
  90.2 5.4 copy-start.43
  90.2 6.0 copy-start.64
  90.2 6.6 %copy-start.35 = (f32[9216]{0:T(1024)S(1)}, f32[9216]{0:T(1024)}, u32[]{:S(2)}) copy-start(f32[9216]{0:T(1024)} %param.28) | copy-start | bytes 110596
  90.2 7.2 %copy-start.37 = (f32[6,1024]{1,0:T(8,128)S(1)}, f32[6,1024]{1,0:T(8,128)}, u32[]{:S(2)}) copy-start(f32[6,1024]{1,0:T(8,128)} %param.27) | copy-start | bytes 73732
  198.6 5.0 slice-start.10
  199.2 4.7 slice-start.11
  200.7 10.0 %copy-start.5 = (bf16[1024,1024]{1,0:T(8,128)(2,1)}, bf16[1024,1024]{1,0:T(8,128)(2,1)S(1)}, u32[]{:S(2)}) copy-start(bf16[1024,1024]{1,0:T(8,128)(2,1)S(1)} %add_convert_fusion.1) | copy-start | bytes 6291460
  202.7 8.0 %copy-start.20 = (bf16[128,1024]{1,0:T(8,128)(2,1)}, bf16[128,1024]{1,0:T(8,128)(2,1)S(1)}, u32[]{:S(2)}) copy-start(bf16[128,1024]{1,0:T(8,128)(2,1)S(1)} %convolution_convert_fusion) | copy-start | bytes 786436
  203.3 8.3 %copy-start.29 = (bf16[1024,12]{0,1:T(8,128)(2,1)}, bf16[1024,12]{0,1:T(8,128)(2,1)S(1)}, u32[]{:S(2)}) copy-start(bf16[1024,12]{0,1:T(8,128)(2,1)S(1)} %convolution_convert_fusion.1) | copy-start | bytes 73732
  203.9 7.3 %copy-start.53 = (bf16[128,12]{0,1:T(8,128)(2,1)}, bf16[128,12]{0,1:T(8,128)(2,1)S(1)}, u32[]{:S(2)}) copy-start(bf16[128,12]{0,1:T(8,128)(2,1)S(1)} %fusion.61) | copy-start | bytes 9220
  211.6 19.3 %copy-start.21 = (bf16[128,1024]{0,1:T(8,128)(2,1)}, bf16[128,1024]{0,1:T(8,128)(2,1)S(1)}, u32[]{:S(2)}) copy-start(bf16[128,1024]{0,1:T(8,128)(2,1)S(1)} %copy.45) | copy-start | bytes 786436
  221.8 9.1 %copy-start.7 = (bf16[1024,1024]{0,1:T(8,128)(2,1)}, bf16[1024,1024]{0,1:T(8,128)(2,1)S(1)}, u32[]{:S(2)}) copy-start(bf16[1024,1024]{0,1:T(8,128)(2,1)S(1)} %copy.44) | copy-start | bytes 6291460
  237.2 8.5 %slice-start.2 = ((s8[8388608]{0:T(1024)(128)(4,1)}), s8[4194304]{0:T(1024)(128)(4,1)S(1)}, s32[]{:S(2)}) async-start(s8[8388608]{0:T(1024)(128)(4,1)} %bitcast.163), calls=%async_computation.8 | async-start | bytes 8388608
  237.8 6.2 %copy-start.11 = (bf16[1024,4]{1,0:T(8,128)(2,1)S(1)}, bf16[1024,4]{1,0:T(8,128)(2,1)}, u32[]{:S(2)}) copy-start(bf16[1024,4]{1,0:T(8,128)(2,1)} %convert_element_type.200) | copy-start | bytes 24580
  237.8 6.4 %copy-start.9 = (bf16[1024,1024]{1,0:T(8,128)(2,1)S(1)}, bf16[1024,1024]{1,0:T(8,128)(2,1)}, u32[]{:S(2)}) copy-start(bf16[1024,1024]{1,0:T(8,128)(2,1)} %param.24) | copy-start | bytes 6291460
  237.8 6.4 %copy-start.17 = (f32[128,1024]{1,0:T(8,128)S(1)}, f32[128,1024]{1,0:T(8,128)}, u32[]{:S(2)}) copy-start(f32[128,1024]{1,0:T(8,128)} %gather_fusion.2) | copy-start | bytes 1572868
  237.8 6.4 %copy-start.41 = (f32[1024]{0:T(1024)S(1)}, f32[1024]{0:T(1024)}, u32[]{:S(2)}) copy-start(f32[1024]{0:T(1024)} %get-tuple-element.40) | copy-start | bytes 12292
  237.8 6.4 %copy-start.61 = (pred[128]{0:T(512)(128)(4,1)S(1)}, pred[128]{0:T(512)(128)(4,1)}, u32[]{:S(2)}) copy-start(pred[128]{0:T(512)(128)(4,1)} %get-tuple-element.25) | copy-start | bytes 388
  237.8 7.9 %slice-start.3 = ((s8[8388608]{0:T(1024)(128)(4,1)}), s8[4194304]{0:T(1024)(128)(4,1)S(1)}, s32[]{:S(2)}) async-start(s8[8388608]{0:T(1024)(128)(4,1)} %bitcast.163), calls=%async_computation.9 | async-start | bytes 8388608
  244.2 5.8 slice-start
  245.8 4.3 slice-start.1
  251.9 52.6 %copy-start.51 = (f32[128]{0:T(128)}, f32[128]{0:T(128)S(1)}, u32[]{:S(2)}) copy-start(f32[128]{0:T(128)S(1)} %broadcast_multiply_fusion.2) | copy-start | bytes 1540
  252.1 9.8 %copy-start.67 = (f32[128]{0:T(128)}, f32[128]{0:T(128)S(1)}, u32[]{:S(2)}) copy-start(f32[128]{0:T(128)S(1)} %multiply_reduce_fusion.4) | copy-start | bytes 1540
  252.1 9.8 %copy-start.59 = (f32[128]{0:T(128)}, f32[128]{0:T(128)S(1)}, u32[]{:S(2)}) copy-start(f32[128]{0:T(128)S(1)} %fusion.80) | copy-start | bytes 1540
  253.0 191.5 %reduce-scatter.5.cloned.1.call-start = ((), (), s32[]{:S(2)}) async-start(), calls=%async_computation.4 | async-start | bytes 4718592 | tf_op jit(solution)/shard_map/reduce_scatter | solution.py:246
  392.3 52.2 %copy-start.52 = (f32[128]{0:T(128)S(1)}, f32[128]{0:T(128)}, u32[]{:S(2)}) copy-start(f32[128]{0:T(128)} %copy-done.51) | copy-start | bytes 1540
  392.3 53.8 %copy-start.68 = (f32[128]{0:T(128)S(1)}, f32[128]{0:T(128)}, u32[]{:S(2)}) copy-start(f32[128]{0:T(128)} %copy-done.67) | copy-start | bytes 1540
  392.3 53.8 %copy-start.60 = (f32[128]{0:T(128)S(1)}, f32[128]{0:T(128)}, u32[]{:S(2)}) copy-start(f32[128]{0:T(128)} %copy-done.59) | copy-start | bytes 1540
  392.3 184.5 %all-gather.7.cloned.1.call-start = ((), (), s32[]{:S(2)}) async-start(), calls=%async_computation.5 | async-start | bytes 9732096 | tf_op jit(solution)/shard_map/all_gather | solution.py:314
  447.4 8.2 %copy-start.69 = (f32[128,4096]{1,0:T(8,128)S(1)}, f32[128,4096]{1,0:T(8,128)}, u32[]{:S(2)}) copy-start(f32[128,4096]{1,0:T(8,128)} %get-tuple-element.58) | copy-start | bytes 6291460
  447.4 10.6 %slice-start.4 = ((s8[8388608]{0:T(1024)(128)(4,1)}), s8[4194304]{0:T(1024)(128)(4,1)S(1)}, s32[]{:S(2)}) async-start(s8[8388608]{0:T(1024)(128)(4,1)} %bitcast.165), calls=%async_computation.10 | async-start | bytes 8388608
  464.6 5.9 copy-start.27
  464.6 5.9 slice-start.6
  464.6 6.5 %slice-start.7 = ((s8[8388608]{0:T(1024)(128)(4,1)}), s8[4194304]{0:T(1024)(128)(4,1)S(1)}, s32[]{:S(2)}) async-start(s8[8388608]{0:T(1024)(128)(4,1)} %bitcast.171), calls=%async_computation.13 | async-start | bytes 8388608
  478.7 5.4 copy-start.30
  478.8 9.7 %copy-start.6 = (bf16[1024,1024]{1,0:T(8,128)(2,1)S(1)}, bf16[1024,1024]{1,0:T(8,128)(2,1)}, u32[]{:S(2)}) copy-start(bf16[1024,1024]{1,0:T(8,128)(2,1)} %copy-done.5) | copy-start | bytes 6291460
  480.2 8.3 %copy-start.36 = (bf16[4,1024]{1,0:T(4,128)(2,1)S(1)}, bf16[4,1024]{1,0:T(4,128)(2,1)}, u32[]{:S(2)}) copy-start(bf16[4,1024]{1,0:T(4,128)(2,1)} %squeeze.25) | copy-start | bytes 24580
  488.6 5.3 copy-start.34
  488.6 5.3 copy-start.33
  576.9 15.4 %copy-start.1 = (bf16[1024,1024]{1,0:T(8,128)(2,1)S(1)}, bf16[1024,1024]{1,0:T(8,128)(2,1)}, u32[]{:S(2)}) copy-start(bf16[1024,1024]{1,0:T(8,128)(2,1)} %param.22) | copy-start | bytes 6291460
  585.1 6.1 %copy-start.19 = (f32[73728]{0:T(1024)S(1)}, f32[73728]{0:T(1024)}, u32[]{:S(2)}) copy-start(f32[73728]{0:T(1024)} %param.29) | copy-start | bytes 884740
  585.1 6.1 %copy-start.25 = (f32[73728]{0:T(1024)S(1)}, f32[73728]{0:T(1024)}, u32[]{:S(2)}) copy-start(f32[73728]{0:T(1024)} %param.30) | copy-start | bytes 884740
  585.1 6.1 %copy-start.26 = (f32[73728]{0:T(1024)S(1)}, f32[73728]{0:T(1024)}, u32[]{:S(2)}) copy-start(f32[73728]{0:T(1024)} %param.31) | copy-start | bytes 884740
  (38 other events, 81.3 us)
Sparse Core Ops, SparseCore 0:
  79.3 116.0 reduce-scatter.2
  253.1 27.8 all-gather.4
  392.5 51.9 reduce-scatter.4
  494.8 82.0 all-gather.6
